TPU v7x, 32 devices: a whole 2x2x4 slice. The times are simulated.
32 devices in a mesh: replica: 4 (over x, core), fsdp: 8 (over z, y).
Axes of the slice: x: 2, y: 2, z: 4, core: 2. Of those that a mesh axis runs over, the one named last changes fastest.
Arguments:
- tokens: bfloat16 [32768, 768], P(('replica', 'fsdp')), may hold values from -6 to 6
- lengths: int32 [32], P(('replica', 'fsdp')), may hold values from 513 to 1024, as said below
- random_blocks: int32 [32, 16, 3], P(('replica', 'fsdp')), may hold values from 0 to 15, as said below
- qkv_weight: bfloat16 [768, 2304], P('fsdp'), may hold values from -0.21875 to 0.21875
- out_weight: bfloat16 [768, 768], P('fsdp'), may hold values from -1.75 to 1.75
- up_weight: bfloat16 [768, 3072], P('fsdp'), may hold values from -0.21875 to 0.21875
- down_weight: bfloat16 [3072, 768], P('fsdp'), may hold values from -0.109375 to 0.109375
- proj_bias: bfloat16 [4, 768], P(None, 'fsdp'), may hold values from -3 to 3
- up_bias: bfloat16 [3072], P('fsdp'), may hold values from -3 to 3
- norm_gain: bfloat16 [2, 768], P(None, 'fsdp'), may hold values from 0.5 to 1.5
- norm_bias: bfloat16 [2, 768], P(None, 'fsdp'), may hold values from -3 to 3
- cotangent: bfloat16 [32768, 768], P(('replica', 'fsdp')), may hold values from -6 to 6
Outputs:
- out: bfloat16 [32768, 768], P(('replica', 'fsdp'))
- input_grad: float32 [32768, 768], P(('replica', 'fsdp'))
- qkv_grad: float32 [768, 2304], P('fsdp')
- out_weight_grad: float32 [768, 768], P('fsdp')
- up_grad: float32 [768, 3072], P('fsdp')
- down_grad: float32 [3072, 768], P('fsdp')
- proj_bias_grad: float32 [4, 768], P(None, 'fsdp')
- up_bias_grad: float32 [3072], P('fsdp')
- gain_grad: float32 [2, 768], P(None, 'fsdp')
- norm_bias_grad: float32 [2, 768], P(None, 'fsdp')
Inputs may be any that keep to these rules, and one draw needn't show every extreme that they name: Slot s holds one sequence of lengths[s] positions from its start; the rest is padding. Each entry of random_blocks[s] is below ceil(lengths[s] / 64), so random blocks lie inside the sequence.
All inputs are finite; a program needn't handle non-finite values.
Results may differ from a plain program's by a relative error of at most 0.017.
Values may be sent and summed in bfloat16 or wider, within the bound.
No kernel may reach another device: no remote copies, remote signals or barrier semaphores. Data moves between devices by JAX's collectives and lax.ppermute only.
A program may use at most 256 MiB of HBM per device.

v0:
```python
import math
import jax
import jax.numpy as jnp
from jax import lax
from jax.sharding import PartitionSpec as P

D = 768
H = 12
HD = 64
BLK = 64
norm_eps = 1e-06


def as_sent(array):
    return jax.tree.map(lambda a: a.astype(jnp.bfloat16) if a.dtype == jnp.float32 else a, array)


def layer_norm(hidden, factor, offset):
    centre = hidden - jnp.mean(hidden, axis=-1, keepdims=True)
    variance = jnp.mean(centre * centre, axis=-1, keepdims=True)
    return centre * lax.rsqrt(variance + norm_eps) * factor + offset


def gelu_tanh(values):
    return jax.nn.gelu(values, approximate=True)


def block_mask(length, chosen, seq_len, block_size):
    block_count = chosen.shape[0]
    blocks_used = (length + block_size - 1) // block_size
    query_block = jnp.arange(block_count, dtype=jnp.int32)[:, None]
    key_block = jnp.arange(block_count, dtype=jnp.int32)[None, :]
    nearby = jnp.abs(query_block - key_block) <= 1
    global_key = (key_block == 0) | (key_block == blocks_used - 1)
    global_query = (query_block == 0) | (query_block == blocks_used - 1)
    picked = jnp.any(chosen[:, None, :] == key_block[:, :, None], axis=2)
    allowed = (nearby | global_key | global_query | picked) & (key_block < blocks_used)
    spread_mask = jnp.repeat(jnp.repeat(allowed, block_size, axis=0), block_size, axis=1)
    key_pos = jnp.arange(seq_len, dtype=jnp.int32)[None, :]
    return spread_mask & (key_pos < length)


def masked_scores(query_block, mask_block, keys, scale):
    scores = (
        jnp.einsum("qhd,khd->hqk", query_block, keys, preferred_element_type=jnp.float32) * scale
    )
    return jnp.where(mask_block[None], scores, -1000000000.0)


def forward_block(query_block, mask_block, keys, values, scale):
    scores = masked_scores(query_block, mask_block, keys, scale)
    peak = jnp.max(scores, axis=-1, keepdims=True)
    weights = jnp.exp(scores - peak)
    total = jnp.sum(weights, axis=-1, keepdims=True)
    probs = (weights / total).astype(jnp.bfloat16)
    context = jnp.einsum("hqk,khd->qhd", probs, values, preferred_element_type=jnp.float32)
    return (context, peak + jnp.log(total))


def backward_block(query_block, mask_block, grad_block, logsum, keys, values, scale):
    scores = masked_scores(query_block, mask_block, keys, scale)
    probs = jnp.exp(scores - logsum)
    grad_probs = jnp.einsum("qhd,khd->hqk", grad_block, values, preferred_element_type=jnp.float32)
    inner = jnp.sum(grad_probs * probs, axis=-1, keepdims=True)
    grad_scores = (probs * (grad_probs - inner)).astype(jnp.bfloat16)
    grad_query = (
        jnp.einsum("hqk,khd->qhd", grad_scores, keys, preferred_element_type=jnp.float32) * scale
    )
    grad_key = (
        jnp.einsum("hqk,qhd->khd", grad_scores, query_block, preferred_element_type=jnp.float32)
        * scale
    )
    grad_value = jnp.einsum(
        "hqk,qhd->khd", probs.astype(jnp.bfloat16), grad_block, preferred_element_type=jnp.float32
    )
    return (grad_query, grad_key, grad_value)


def shards(
    tokens,
    lengths,
    random_blocks,
    qkv_weight,
    out_weight,
    up_weight,
    down_weight,
    proj_bias,
    up_bias,
    norm_gain,
    norm_bias,
    cotangent,
):
    seq_len = tokens.shape[0]
    length = lengths[0]
    valid = (jnp.arange(seq_len, dtype=jnp.int32) < length).astype(jnp.float32)[:, None]
    allowed = block_mask(length, random_blocks[0], seq_len, BLK)
    scale = 1.0 / math.sqrt(HD)
    rows_step = min(512, seq_len)
    gathered = (
        lax.all_gather(qkv_weight, "fsdp", axis=0, tiled=True),
        lax.all_gather(out_weight, "fsdp", axis=0, tiled=True),
        lax.all_gather(up_weight, "fsdp", axis=0, tiled=True),
        lax.all_gather(down_weight, "fsdp", axis=0, tiled=True),
        lax.all_gather(proj_bias, "fsdp", axis=1, tiled=True),
        lax.all_gather(up_bias, "fsdp", axis=0, tiled=True),
        lax.all_gather(norm_gain, "fsdp", axis=1, tiled=True),
        lax.all_gather(norm_bias, "fsdp", axis=1, tiled=True),
    )
    qkv_full, out_full, bias_full = (gathered[0], gathered[1], gathered[4])
    early_mlp = (gathered[2], gathered[3], gathered[5], gathered[6], gathered[7])
    mixed = jnp.dot(tokens, qkv_full, preferred_element_type=jnp.float32)
    queries = (mixed[:, :D] + bias_full[0]).astype(jnp.bfloat16).reshape(seq_len, H, HD)
    keys = mixed[:, D : 2 * D].astype(jnp.bfloat16).reshape(seq_len, H, HD)
    values = (mixed[:, 2 * D :] + bias_full[1]).astype(jnp.bfloat16).reshape(seq_len, H, HD)
    contexts = []
    logsums = []
    for begin_row in range(0, seq_len, rows_step):
        context, logsum = forward_block(
            queries[begin_row : begin_row + rows_step],
            allowed[begin_row : begin_row + rows_step],
            keys,
            values,
            scale,
        )
        contexts.append(context)
        logsums.append(logsum)
    context_low = jnp.concatenate(contexts, axis=0).reshape(seq_len, D).astype(jnp.bfloat16)
    branch = jnp.dot(context_low, out_full, preferred_element_type=jnp.float32) + bias_full[2]
    up_full, down_full, up_bias_full, gain_full, shift_full = early_mlp
    gain_float = gain_full.astype(jnp.float32)
    shift_float = shift_full.astype(jnp.float32)
    hidden_one = tokens.astype(jnp.float32) + branch
    normed, first_pull = jax.vjp(layer_norm, hidden_one, gain_float[0], shift_float[0])
    normed_low = normed.astype(jnp.bfloat16)
    upward = jnp.dot(normed_low, up_full, preferred_element_type=jnp.float32) + up_bias_full
    activated, gelu_pull = jax.vjp(gelu_tanh, upward)
    activated_low = activated.astype(jnp.bfloat16)
    downward = jnp.dot(activated_low, down_full, preferred_element_type=jnp.float32) + bias_full[3]
    final_norm, second_pull = jax.vjp(layer_norm, normed + downward, gain_float[1], shift_float[1])
    result = (final_norm * valid).astype(jnp.bfloat16)
    qkv_back, out_back, up_back, down_back = (
        lax.all_gather(qkv_weight, "fsdp", axis=0, tiled=True),
        lax.all_gather(out_weight, "fsdp", axis=0, tiled=True),
        lax.all_gather(up_weight, "fsdp", axis=0, tiled=True),
        lax.all_gather(down_weight, "fsdp", axis=0, tiled=True),
    )
    grad_out = cotangent.astype(jnp.float32) * valid
    grad_two, gain_two, shift_two = second_pull(grad_out)
    grad_down = grad_two.astype(jnp.bfloat16)
    down_grad = jnp.einsum(
        "sf,sd->fd", activated_low, grad_down, preferred_element_type=jnp.float32
    )
    grad_act = jnp.einsum("sd,fd->sf", grad_down, down_back, preferred_element_type=jnp.float32)
    grad_up = gelu_pull(grad_act)[0].astype(jnp.bfloat16)
    up_grad = jnp.einsum("sd,sf->df", normed_low, grad_up, preferred_element_type=jnp.float32)
    up_bias_grad = jnp.sum(grad_up, axis=0, dtype=jnp.float32)
    grad_normed = grad_two + jnp.einsum(
        "sf,df->sd", grad_up, up_back, preferred_element_type=jnp.float32
    )
    grad_one, gain_one, shift_one = first_pull(grad_normed)
    grad_branch = grad_one.astype(jnp.bfloat16)
    out_grad = jnp.einsum("sd,se->de", context_low, grad_branch, preferred_element_type=jnp.float32)
    grad_context = (
        jnp.einsum("se,de->sd", grad_branch, out_back, preferred_element_type=jnp.float32)
        .astype(jnp.bfloat16)
        .reshape(seq_len, H, HD)
    )
    query_parts = []
    key_total = jnp.zeros((seq_len, H, HD), jnp.float32)
    value_total = jnp.zeros((seq_len, H, HD), jnp.float32)
    for block_index, begin_row in enumerate(range(0, seq_len, rows_step)):
        grad_query, grad_key, grad_value = backward_block(
            queries[begin_row : begin_row + rows_step],
            allowed[begin_row : begin_row + rows_step],
            grad_context[begin_row : begin_row + rows_step],
            logsums[block_index],
            keys,
            values,
            scale,
        )
        query_parts.append(grad_query)
        key_total = key_total + grad_key
        value_total = value_total + grad_value
    grad_queries = jnp.concatenate(query_parts, axis=0).reshape(seq_len, D).astype(jnp.bfloat16)
    grad_keys = key_total.reshape(seq_len, D).astype(jnp.bfloat16)
    grad_values = value_total.reshape(seq_len, D).astype(jnp.bfloat16)
    grad_mixed = jnp.concatenate([grad_queries, grad_keys, grad_values], axis=1)
    qkv_grad = jnp.einsum("sd,se->de", tokens, grad_mixed, preferred_element_type=jnp.float32)
    input_grad = grad_one + jnp.einsum(
        "se,de->sd", grad_mixed, qkv_back, preferred_element_type=jnp.float32
    )
    bias_grads = jnp.stack(
        [
            jnp.sum(grad_queries, axis=0, dtype=jnp.float32),
            jnp.sum(grad_values, axis=0, dtype=jnp.float32),
            jnp.sum(grad_branch, axis=0, dtype=jnp.float32),
            jnp.sum(grad_down, axis=0, dtype=jnp.float32),
        ]
    )
    gain_grads = jnp.stack([gain_one, gain_two])
    shift_grads = jnp.stack([shift_one, shift_two])
    shares = (
        lax.psum_scatter(qkv_grad, "fsdp", scatter_dimension=0, tiled=True),
        lax.psum_scatter(out_grad, "fsdp", scatter_dimension=0, tiled=True),
        lax.psum_scatter(up_grad, "fsdp", scatter_dimension=0, tiled=True),
        lax.psum_scatter(down_grad, "fsdp", scatter_dimension=0, tiled=True),
        lax.psum_scatter(bias_grads, "fsdp", scatter_dimension=1, tiled=True),
        lax.psum_scatter(up_bias_grad, "fsdp", scatter_dimension=0, tiled=True),
        lax.psum_scatter(gain_grads, "fsdp", scatter_dimension=1, tiled=True),
        lax.psum_scatter(shift_grads, "fsdp", scatter_dimension=1, tiled=True),
    )
    totals = jax.tree.map(
        lambda part: part.astype(jnp.float32), lax.psum(as_sent(tuple(shares)), "replica")
    )
    return (
        result,
        input_grad,
        totals[0],
        totals[1],
        totals[2],
        totals[3],
        totals[4],
        totals[5],
        totals[6],
        totals[7],
    )


def solution(mesh):
    return jax.shard_map(
        shards,
        mesh=mesh,
        in_specs=(
            P(("replica", "fsdp"), None),
            P(("replica", "fsdp")),
            P(("replica", "fsdp"), None, None),
            P("fsdp", None),
            P("fsdp", None),
            P("fsdp", None),
            P("fsdp", None),
            P(None, "fsdp"),
            P("fsdp"),
            P(None, "fsdp"),
            P(None, "fsdp"),
            P(("replica", "fsdp"), None),
        ),
        out_specs=(
            P(("replica", "fsdp"), None),
            P(("replica", "fsdp"), None),
            P("fsdp", None),
            P("fsdp", None),
            P("fsdp", None),
            P("fsdp", None),
            P(None, "fsdp"),
            P("fsdp"),
            P(None, "fsdp"),
            P(None, "fsdp"),
        ),
        check_vma=False,
    )
```

profile of v0, /device:TPU:0, one launch (start us, length us, event | category | flops | bytes accessed | tf_op | source)
XLA Modules:
  0.0 1199.1 jit_solution(17224826126633601862)
XLA Ops:
  12.9 22.3 %all-gather.1 = bf16[8,96,2]{1,2,0:T(2,128)(2,1)S(1)} all-gather(bf16[1,96,2]{1,2,0:T(2,128)(2,1)} %bitcast.138), channel_id=1, replica_groups=mesh['replica'=4,'fsdp'=8] {'fsdp'}, dimensions={0}, use_global_device_ids=true | all-gather | bytes 3456 | tf_op jit(solution)/shard_map/all_gather | solution.py:106
  35.3 16.4 %all-gather.2 = bf16[8,96,2]{1,2,0:T(2,128)(2,1)S(1)} all-gather(bf16[1,96,2]{1,2,0:T(2,128)(2,1)} %bitcast.139), channel_id=1, replica_groups=mesh['replica'=4,'fsdp'=8] {'fsdp'}, dimensions={0}, use_global_device_ids=true | all-gather | bytes 3456 | tf_op jit(solution)/shard_map/all_gather | solution.py:107
  51.9 18.6 %all-gather = bf16[8,96,4]{1,2,0:T(4,128)(2,1)S(1)} all-gather(bf16[1,96,4]{1,2,0:T(4,128)(2,1)} %bitcast.137), channel_id=1, replica_groups=mesh['replica'=4,'fsdp'=8] {'fsdp'}, dimensions={0}, use_global_device_ids=true | all-gather | bytes 6912 | tf_op jit(solution)/shard_map/all_gather | solution.py:104
  71.2 25.9 %all-gather.3 = bf16[8,1,384]{2,1,0:T(2,128)(2,1)S(1)} all-gather(bf16[1,1,384]{2,1,0:T(2,128)(2,1)S(1)} %reshape.199), channel_id=1, replica_groups=mesh['replica'=4,'fsdp'=8] {'fsdp'}, dimensions={0}, use_global_device_ids=true | all-gather | bytes 6912 | tf_op jit(solution)/shard_map/all_gather | solution.py:105
  101.8 1.6 copy.104
  103.5 2.8 copy.93
  106.9 5.8 fusion.67
  112.7 3.6 copy-done.17
  117.3 5.1 fusion.21
  124.8 1.7 copy.95
  126.5 12.6 %fusion.20 = (f32[12,512]{1,0:T(8,128)S(1)}, f32[12,512,1024]{2,1,0:T(8,128)}) fusion(pred[512,1024]{1,0:T(8,128)(4,1)} %copy.100, bf16[512,12,64]{0,2,1:T(8,128)(2,1)} %bitcast.108, bf16[1024,12,64]{0,2,1:T(8,128)(2,1)S(1)} %bitcast.100), kind=kOutput, calls=%fused_computation.34 | convolution fusion | flops 824174592 | bytes 28073984 | tf_op jit(solution)/shard_map/qhd,khd->hqk/dot_general | solution.py:45
  139.2 12.4 %fusion.1 = f32[12,512]{1,0:T(8,128)S(1)} fusion(f32[12,512]{1,0:T(8,128)S(1)} %get-tuple-element.103, f32[12,512,1024]{2,1,0:T(8,128)} %get-tuple-element.104, pred[512,1024]{1,0:T(8,128)(4,1)S(1)} %copy-done.13), kind=kLoop, calls=%fused_computation.13 | loop fusion | flops 25159680 | bytes 25739264 | tf_op jit(solution)/shard_map/reduce_sum | solution.py:54
  151.6 3.1 copy-done.1
  154.7 8.4 fusion.32
  163.1 12.2 %fusion.19 = (f32[12,512]{1,0:T(8,128)S(1)}, f32[12,512,1024]{2,1,0:T(8,128)}) fusion(pred[512,1024]{1,0:T(8,128)(4,1)S(1)} %copy-done.10, bf16[512,12,64]{0,2,1:T(8,128)(2,1)} %bitcast.110, bf16[1024,12,64]{0,2,1:T(8,128)(2,1)S(1)} %bitcast.101), kind=kOutput, calls=%fused_computation.33 | convolution fusion | flops 824174592 | bytes 28073984 | tf_op jit(solution)/shard_map/qhd,khd->hqk/dot_general | solution.py:45
  175.3 12.4 %fusion = f32[12,512]{1,0:T(8,128)S(1)} fusion(f32[12,512]{1,0:T(8,128)S(1)} %get-tuple-element.105, f32[12,512,1024]{2,1,0:T(8,128)} %get-tuple-element.106, pred[512,1024]{1,0:T(8,128)(4,1)S(1)} %copy-done.10), kind=kLoop, calls=%fused_computation.12 | loop fusion | flops 25159680 | bytes 25739264 | tf_op jit(solution)/shard_map/reduce_sum | solution.py:54
  187.8 3.2 copy-done
  190.9 7.8 fusion.31
  200.1 3.8 fusion.65
  204.4 11.2 fusion.57
  215.6 65.6 %all-gather.15.cloned.1.call-done = bf16[3072,768]{1,0:T(8,128)(2,1)} async-done(((bf16[384,768]{1,0:T(8,128)(2,1)}), bf16[3072,768]{1,0:T(8,128)(2,1)}) %all-gather.15.cloned.1.call-update) | async-done | bytes 4718608 | tf_op jit(solution)/shard_map/all_gather | solution.py:103
  281.2 11.7 fusion.66
  293.0 1.7 multiply_reduce_fusion.5
  294.7 2.1 multiply_reduce_fusion.2
  296.8 3.6 convert_reduce_fusion.1
  300.4 18.1 %convert_reduce_fusion = (f32[3072]{0:T(1024)}, bf16[1024,3072]{1,0:T(8,128)(2,1)}) fusion(f32[1024,3072]{1,0:T(8,128)} %fusion.57, f32[3072]{0:T(1024)S(1)} %bitcast.134, bf16[1024,768]{0,1:T(8,128)(2,1)S(1)} %get-tuple-element.89, bf16[3072,768]{1,0:T(8,128)(2,1)} %all-gather.15.cloned.1.call-done), kind=kOutput, calls=%fused_computation.27 | convolution fusion | flops 4904186880 | bytes 25190400 | tf_op jit(solution)/shard_map/sd,fd->sf/dot_general | solution.py:153
  318.4 9.8 multiply_reduce_fusion.3
  329.1 1.6 copy-done.15
  331.7 2.8 fusion.69
  337.7 21.3 %multiply_reduce_fusion.1 = (f32[12,512]{1,0:T(8,128)S(1)}, f32[12,512,1024]{2,1,0:T(8,128)}) fusion(f32[12,512]{1,0:T(8,128)S(1)} %log_add_fusion.1, f32[12,512,1024]{2,1,0:T(8,128)} %get-tuple-element.106, pred[512,1024]{1,0:T(8,128)(4,1)S(1)} %copy-done.11, bf16[512,12,64]{0,2,1:T(8,128)(2,1)S(1)} %bitcast.116, bf16[1024,12,64]{0,2,1:T(8,128)(2,1)S(1)} %bitcast.106), kind=kOutput, calls=%fused_computation.4 | convolution fusion | flops 836757504 | bytes 53264384 | tf_op jit(solution)/shard_map/qhd,khd->hqk/dot_general | solution.py:63
  359.0 17.4 %multiply_convert_fusion.1 = bf16[12,512,1024]{2,1,0:T(8,128)(2,1)S(1)} fusion(f32[12,512,1024]{2,1,0:T(8,128)} %get-tuple-element.113, f32[12,512]{1,0:T(8,128)S(1)} %get-tuple-element.112, f32[12,512]{1,0:T(8,128)S(1)} %log_add_fusion.1, f32[12,512,1024]{2,1,0:T(8,128)} %get-tuple-element.106, pred[512,1024]{1,0:T(8,128)(4,1)} %copy.97), kind=kLoop, calls=%fused_computation.3 | loop fusion | flops 37748736 | bytes 63488000 | tf_op jit(solution)/shard_map/convert_element_type | solution.py:65
  376.4 6.2 multiply_bitcast_fusion.1
  382.6 5.0 fusion.68
  389.1 17.8 %multiply_reduce_fusion = (f32[12,512]{1,0:T(8,128)S(1)}, f32[12,512,1024]{2,1,0:T(8,128)}) fusion(f32[12,512]{1,0:T(8,128)S(1)} %log_add_fusion, f32[12,512,1024]{2,1,0:T(8,128)} %get-tuple-element.104, pred[512,1024]{1,0:T(8,128)(4,1)} %copy.100, bf16[512,12,64]{0,2,1:T(8,128)(2,1)} %bitcast.118, bf16[1024,12,64]{0,2,1:T(8,128)(2,1)S(1)} %bitcast.107), kind=kOutput, calls=%fused_computation.1 | convolution fusion | flops 836757504 | bytes 53264384 | tf_op jit(solution)/shard_map/qhd,khd->hqk/dot_general | solution.py:63
  406.9 17.7 %multiply_convert_fusion = bf16[12,512,1024]{2,1,0:T(8,128)(2,1)S(1)} fusion(f32[12,512,1024]{2,1,0:T(8,128)} %get-tuple-element.115, f32[12,512]{1,0:T(8,128)S(1)} %get-tuple-element.114, f32[12,512]{1,0:T(8,128)S(1)} %log_add_fusion, f32[12,512,1024]{2,1,0:T(8,128)} %get-tuple-element.104, pred[512,1024]{1,0:T(8,128)(4,1)} %copy.100), kind=kLoop, calls=%fused_computation | loop fusion | flops 37748736 | bytes 63488000 | tf_op jit(solution)/shard_map/convert_element_type | solution.py:65
  424.6 6.2 multiply_bitcast_fusion
  430.8 2.9 convert_reduce_fusion.4
  433.7 4.7 multiply_convert_fusion.3
  438.5 12.0 %fusion.11 = f32[12,64,1024]{2,1,0:T(8,128)S(1)} fusion(bf16[512,12,64]{0,2,1:T(8,128)(2,1)S(1)} %bitcast.119, f32[12,512]{1,0:T(8,128)S(1)} %log_add_fusion, f32[12,512,1024]{2,1,0:T(8,128)} %get-tuple-element.104, pred[512,1024]{1,0:T(8,128)(4,1)S(1)} %copy-done.14), kind=kOutput, calls=%fused_computation.25 | convolution fusion | flops 830472192 | bytes 29646848 | tf_op jit(solution)/shard_map/hqk,qhd->khd/dot_general | solution.py:73
  450.5 12.1 %convert_reduce_fusion.3 = (f32[12,64]{1,0:T(8,128)S(1)}, bf16[12,64,1024]{2,1,0:T(8,128)(2,1)S(1)}) fusion(f32[12,64,1024]{2,1,0:T(8,128)S(1)} %fusion.11, bf16[512,12,64]{0,2,1:T(8,128)(2,1)S(1)} %bitcast.117, f32[12,512]{1,0:T(8,128)S(1)} %log_add_fusion.1, f32[12,512,1024]{2,1,0:T(8,128)} %get-tuple-element.106, pred[512,1024]{1,0:T(8,128)(4,1)S(1)} %copy-done.12), kind=kOutput, calls=%fused_computation.50 | convolution fusion | flops 833617152 | bytes 31222784 | tf_op jit(solution)/shard_map/hqk,qhd->khd/dot_general | solution.py:73
  463.8 9.1 convolution_bitcast_fusion
  472.9 8.0 copy.112
  481.0 1.8 copy-done.4
  482.8 10.5 fusion.55
  494.7 14.1 %fusion.60 = f32[3072,768]{1,0:T(8,128)} fusion(bf16[1024,768]{0,1:T(8,128)(2,1)S(1)} %copy-done.29, f32[1024,3072]{1,0:T(8,128)} %fusion.57, f32[3072]{0:T(1024)S(1)} %bitcast.135), kind=kOutput, calls=%fused_computation.134 | convolution fusion | flops 4863295488 | bytes 23605248 | tf_op jit(solution)/shard_map/sf,sd->fd/dot_general | solution.py:150
  514.2 1.6 copy.107
  515.7 1.6 convert_element_type.205
  517.4 90.6 %reduce-scatter.22.cloned.1.call-done = f32[96,2304]{1,0:T(8,128)} async-done(((f32[768,2304]{1,0:T(8,128)}), f32[96,2304]{1,0:T(8,128)}) %reduce-scatter.22.cloned.1.call-update) | async-done | bytes 884752
  608.0 2.2 copy.113
  610.2 164.4 %reduce-scatter.18.cloned.1.call-done = f32[96,3072]{1,0:T(8,128)} async-done(((f32[768,3072]{1,0:T(8,128)}), f32[96,3072]{1,0:T(8,128)}) %reduce-scatter.18.cloned.1.call-update) | async-done | bytes 1179664 | tf_op jit(solution)/shard_map/reduce_scatter | solution.py:205
  774.6 2.2 convert_element_type.207
  776.7 164.4 %reduce-scatter.20.cloned.1.call-done = f32[384,768]{1,0:T(8,128)} async-done(((f32[3072,768]{1,0:T(8,128)}), f32[384,768]{1,0:T(8,128)}) %reduce-scatter.20.cloned.1.call-update) | async-done | bytes 1179664 | tf_op jit(solution)/shard_map/reduce_scatter | solution.py:206
  941.2 2.1 convert_element_type.209
  943.3 8.9 add_add_fusion.4
  952.2 3.6 copy.108
  955.8 35.2 %all-reduce = bf16[3072]{0:T(1024)(128)(2,1)S(1)} all-reduce(f32[3072]{0:T(1024)S(1)} %copy-done.43), channel_id=7, replica_groups=mesh['replica'=4,'fsdp'=8] {'fsdp'}, use_global_device_ids=true, to_apply=%region_30.31.clone | all-reduce | flops 3072 | bytes 18432
  991.1 14.3 %reduce-scatter.28.cloned.1.call-done = f32[96,2]{1,0:T(8,128)} async-done(((f32[768,2]{1,0:T(8,128)}), f32[96,2]{1,0:T(8,128)}) %reduce-scatter.28.cloned.1.call-update) | async-done | bytes 784
  1006.2 63.1 %reduce-scatter.26.cloned.1.call-done = f32[96,2]{1,0:T(8,128)} async-done(((f32[768,2]{1,0:T(8,128)}), f32[96,2]{1,0:T(8,128)}) %reduce-scatter.26.cloned.1.call-update) | async-done | bytes 784
  1070.2 63.2 %reduce-scatter.24.cloned.1.call-done = f32[96,4]{1,0:T(8,128)} async-done(((f32[768,4]{1,0:T(8,128)}), f32[96,4]{1,0:T(8,128)}) %reduce-scatter.24.cloned.1.call-update) | async-done | bytes 1552
  1134.3 5.7 all-reduce.1
  1142.2 42.7 %all-reduce.5.cloned.1.call-done = (bf16[96,2304]{0,1:T(8,128)(2,1)}, bf16[96,768]{1,0:T(8,128)(2,1)}, bf16[96,3072]{1,0:T(8,128)(2,1)}, bf16[384,768]{1,0:T(8,128)(2,1)}) async-done(((bf16[96,2304]{0,1:T(8,128)(2,1)}, bf16[96,768]{1,0:T(8,128)(2,1)}, bf16[96,3072]{1,0:T(8,128)(2,1)}, bf16[384,768]{1,0:T(8,128)(2,1)}), (bf16[96,2304]{0,1:T(8,128)(2,1)}, bf16[96,768]{1,0:T(8,128)(2,1)}, ...) | async-done | bytes 1769488 | tf_op jit(solution)/shard_map/psum | solution.py:213
  1184.9 2.3 copy.109
  1187.2 1.6 convert_element_type.206
  1188.8 2.2 convert_element_type.208
  (199 shorter events, 36.0 us)
Async XLA Ops:
  7.2 99.7 %all-gather.9.cloned.1.call-start = ((), (), s32[]{:S(2)}) async-start(), calls=%async_computation.7 | async-start | bytes 3981312 | tf_op jit(solution)/shard_map/all_gather | solution.py:100
  7.9 192.1 %all-gather.11.cloned.1.call-start = ((), (), s32[]{:S(2)}) async-start(), calls=%async_computation.8 | async-start | bytes 1327104 | tf_op jit(solution)/shard_map/all_gather | solution.py:101
  8.7 195.7 %all-gather.13.cloned.1.call-start = ((), (), s32[]{:S(2)}) async-start(), calls=%async_computation.9 | async-start | bytes 5308416 | tf_op jit(solution)/shard_map/all_gather | solution.py:102
  9.4 92.4 %copy-start.23 = (bf16[1024,768]{1,0:T(8,128)(2,1)S(1)}, bf16[1024,768]{1,0:T(8,128)(2,1)}, u32[]{:S(2)}) copy-start(bf16[1024,768]{1,0:T(8,128)(2,1)} %param.23) | copy-start | bytes 4718596
  9.4 271.8 %all-gather.15.cloned.1.call-start = ((), (), s32[]{:S(2)}) async-start(), calls=%async_computation.10 | async-start | bytes 5308416 | tf_op jit(solution)/shard_map/all_gather | solution.py:103
  10.0 505.8 %reduce-scatter.16.cloned.1.call-start = ((), (), s32[]{:S(2)}) async-start(), calls=%async_computation.11 | async-start | bytes 2654208 | tf_op jit(solution)/shard_map/reduce_scatter | solution.py:204
  103.5 3.4 copy-start.24
  106.9 174.3 %copy-start.32 = (f32[768]{0:T(1024)}, f32[768]{0:T(1024)S(1)}, u32[]{:S(2)}) copy-start(f32[768]{0:T(1024)S(1)} %get-tuple-element.71) | copy-start | bytes 9220
  112.7 3.6 copy-start.17
  117.3 45.8 %copy-start.2 = (bf16[1024,768]{0,1:T(8,128)(2,1)}, bf16[1024,768]{0,1:T(8,128)(2,1)S(1)}, u32[]{:S(2)}) copy-start(bf16[1024,768]{0,1:T(8,128)(2,1)S(1)} %copy.99) | copy-start | bytes 4718596
  126.5 61.2 %copy-start.7 = (bf16[1024,768]{0,1:T(8,128)(2,1)}, bf16[1024,768]{0,1:T(8,128)(2,1)S(1)}, u32[]{:S(2)}) copy-start(bf16[1024,768]{0,1:T(8,128)(2,1)S(1)} %copy.95) | copy-start | bytes 4718596
  126.5 12.7 %copy-start.13 = (pred[512,1024]{1,0:T(8,128)(4,1)S(1)}, pred[512,1024]{1,0:T(8,128)(4,1)}, u32[]{:S(2)}) copy-start(pred[512,1024]{1,0:T(8,128)(4,1)} %copy.100) | copy-start | bytes 1572868
  139.2 15.5 %copy-start.1 = (f32[12,512,1024]{2,1,0:T(8,128)S(1)}, f32[12,512,1024]{2,1,0:T(8,128)}, u32[]{:S(2)}) copy-start(f32[12,512,1024]{2,1,0:T(8,128)} %get-tuple-element.104) | copy-start | bytes 75497472
  154.7 8.4 copy-start.10
  175.3 15.6 %copy-start = (f32[12,512,1024]{2,1,0:T(8,128)S(1)}, f32[12,512,1024]{2,1,0:T(8,128)}, u32[]{:S(2)}) copy-start(f32[12,512,1024]{2,1,0:T(8,128)} %get-tuple-element.106) | copy-start | bytes 75497472
  190.9 7.8 copy-start.30
  203.9 124.4 %copy-start.3 = (f32[1024,768]{0,1:T(8,128)}, f32[1024,768]{0,1:T(8,128)S(1)}, u32[]{:S(2)}) copy-start(f32[1024,768]{0,1:T(8,128)S(1)} %get-tuple-element.108) | copy-start | bytes 9437188
  204.4 76.8 %copy-start.44 = (f32[8,1,384]{2,1,0:T(1,128)S(1)}, f32[8,1,384]{2,1,0:T(1,128)}, u32[]{:S(2)}) copy-start(f32[8,1,384]{2,1,0:T(1,128)} %convert_element_type.226) | copy-start | bytes 36868
  204.4 76.8 %copy-start.46 = (f32[768]{0:T(1024)S(1)}, f32[768]{0:T(1024)}, u32[]{:S(2)}) copy-start(f32[768]{0:T(1024)} %get-tuple-element.72) | copy-start | bytes 9220
  281.2 11.8 copy-start.6
  281.2 11.8 copy-start.34
  281.2 11.8 copy-start.35
  294.7 2.1 copy-start.36
  296.8 21.6 %slice-start = ((s8[4718592]{0:T(1024)(128)(4,1)}), s8[4194304]{0:T(1024)(128)(4,1)S(1)}, s32[]{:S(2)}) async-start(s8[4718592]{0:T(1024)(128)(4,1)} %bitcast.112), calls=%async_computation.19 | async-start | bytes 8388608
  300.4 18.1 %copy-start.28 = (bf16[1024,768]{0,1:T(8,128)(2,1)}, bf16[1024,768]{0,1:T(8,128)(2,1)S(1)}, u32[]{:S(2)}) copy-start(bf16[1024,768]{0,1:T(8,128)(2,1)S(1)} %get-tuple-element.89) | copy-start | bytes 4718596
  300.4 18.1 %slice-start.1 = ((s8[4718592]{0:T(1024)(128)(4,1)}), s8[524288]{0:T(1024)(128)(4,1)S(1)}, s32[]{:S(2)}) async-start(s8[4718592]{0:T(1024)(128)(4,1)} %bitcast.112), calls=%async_computation.20 | async-start | bytes 1048576
  329.1 1.7 copy-start.15
  329.1 2.6 copy-start.27
  329.1 5.4 copy-start.40
  331.7 2.8 copy-start.49
  335.9 1.7 copy-start.8
  335.9 1.8 copy-start.11
  336.9 22.1 %copy-start.20 = (bf16[512,768]{0,1:T(8,128)(2,1)}, bf16[512,768]{0,1:T(8,128)(2,1)S(1)}, u32[]{:S(2)}) copy-start(bf16[512,768]{0,1:T(8,128)(2,1)S(1)} %get-tuple-element.95) | copy-start | bytes 2359300
  387.7 1.4 copy-start.9
  387.7 220.3 %reduce-scatter.22.cloned.1.call-start = ((), (), s32[]{:S(2)}) async-start(), calls=%async_computation.14 | async-start | bytes 7962624
  430.8 2.9 copy-start.5
  433.7 4.7 copy-start.14
  433.7 4.7 copy-start.22
  438.5 12.0 %copy-start.12 = (pred[512,1024]{1,0:T(8,128)(4,1)S(1)}, pred[512,1024]{1,0:T(8,128)(4,1)}, u32[]{:S(2)}) copy-start(pred[512,1024]{1,0:T(8,128)(4,1)} %copy.97) | copy-start | bytes 1572868
  438.5 12.0 %copy-start.21 = (bf16[512,768]{0,1:T(8,128)(2,1)S(1)}, bf16[512,768]{0,1:T(8,128)(2,1)}, u32[]{:S(2)}) copy-start(bf16[512,768]{0,1:T(8,128)(2,1)} %copy-done.20) | copy-start | bytes 2359300
  450.5 13.3 %copy-start.19 = (bf16[12,64,1024]{2,1,0:T(8,128)(2,1)S(1)}, bf16[12,64,1024]{2,1,0:T(8,128)(2,1)}, u32[]{:S(2)}) copy-start(bf16[12,64,1024]{2,1,0:T(8,128)(2,1)} %multiply_convert_fusion.3) | copy-start | bytes 4718596
  450.5 13.2 %copy-start.25 = (bf16[1024,768]{1,0:T(8,128)(2,1)S(1)}, bf16[1024,768]{1,0:T(8,128)(2,1)}, u32[]{:S(2)}) copy-start(bf16[1024,768]{1,0:T(8,128)(2,1)} %param.12) | copy-start | bytes 4718596
  450.5 13.2 %copy-start.26 = (bf16[1024,12,64]{0,2,1:T(8,128)(2,1)S(1)}, bf16[1024,12,64]{0,2,1:T(8,128)(2,1)}, u32[]{:S(2)}) copy-start(bf16[1024,12,64]{0,2,1:T(8,128)(2,1)} %get-tuple-element.85) | copy-start | bytes 4718596
  462.6 1.1 copy-start.50
  480.9 1.9 copy-start.4
  480.9 1.9 copy-start.33
  480.9 293.7 %reduce-scatter.18.cloned.1.call-start = ((), (), s32[]{:S(2)}) async-start(), calls=%async_computation.12 | async-start | bytes 10616832 | tf_op jit(solution)/shard_map/reduce_scatter | solution.py:205
  493.3 1.4 copy-start.29
  493.3 1.4 copy-start.45
  493.3 447.9 %reduce-scatter.20.cloned.1.call-start = ((), (), s32[]{:S(2)}) async-start(), calls=%async_computation.13 | async-start | bytes 10616832 | tf_op jit(solution)/shard_map/reduce_scatter | solution.py:206
  508.8 0.7 copy-start.48
  508.8 0.7 copy-start.47
  508.8 1.8 copy-start.37
  508.8 2.8 copy-start.39
  508.8 4.1 copy-start.51
  508.9 5.3 copy-start.18
  508.9 496.5 %reduce-scatter.28.cloned.1.call-start = ((), (), s32[]{:S(2)}) async-start(), calls=%async_computation.17 | async-start | bytes 442368
  510.5 558.7 %reduce-scatter.26.cloned.1.call-start = ((), (), s32[]{:S(2)}) async-start(), calls=%async_computation.16 | async-start | bytes 442368
  511.8 621.6 %reduce-scatter.24.cloned.1.call-start = ((), (), s32[]{:S(2)}) async-start(), calls=%async_computation.15 | async-start | bytes 442368
  512.9 672.1 %all-reduce.5.cloned.1.call-start = ((), (), s32[]{:S(2)}) async-start(), calls=%async_computation.18 | async-start | bytes 3833856 | tf_op jit(solution)/shard_map/psum | solution.py:213
  517.4 425.9 %copy-start.16 = (f32[1024,768]{0,1:T(8,128)S(1)}, f32[1024,768]{0,1:T(8,128)}, u32[]{:S(2)}) copy-start(f32[1024,768]{0,1:T(8,128)} %copy-done.15) | copy-start | bytes 9437188
  517.4 426.0 %copy-start.41 = (f32[1024]{0:T(1024)S(1)}, f32[1024]{0:T(1024)}, u32[]{:S(2)}) copy-start(f32[1024]{0:T(1024)} %copy-done.40) | copy-start | bytes 12292
  952.2 3.6 copy-start.43
  1184.9 6.1 copy-start.31
  (2 other events, 1.4 us)
Sparse Core Ops, SparseCore 0:
  10.2 68.0 all-gather.8
  80.5 39.7 all-gather.10
  122.4 78.6 all-gather.12
  203.1 78.0 all-gather.14
  387.8 67.3 reduce-scatter.15
  481.0 126.8 reduce-scatter.21
  612.0 162.5 reduce-scatter.17
  778.6 162.5 reduce-scatter.19
  944.8 60.5 reduce-scatter.27
  1008.8 60.4 reduce-scatter.25
  1072.9 60.4 reduce-scatter.23
  1136.6 48.2 all-reduce.4
where the time goes:
time: 1210 us; the launch traced here: 1200 us
  waiting for transfers between devices  671 us (55%)
  matrix products  234 us (19%)
  blocking collectives  124 us (10%)
  other arithmetic  94.4 us (8%)
  local copies, waits for them, and re-layouts  59 us (5%)
  between operations  16.3 us (1%)
    unnamed x16, waiting for transfers between devices  234 us
    reduce_scatter x1, waiting for transfers between devices, shards(): lax.psum_scatter(down_grad, 'fsdp', scatter_dimension=0, tiled=True)  164 us
    reduce_scatter x1, waiting for transfers between devices, shards(): lax.psum_scatter(up_grad, 'fsdp', scatter_dimension=0, tiled=True)  164 us
    all_gather x1, waiting for transfers between devices, shards(): lax.all_gather(down_weight, 'fsdp', axis=0, tiled=True)  65.6 us
    unnamed x126, local copies, waits for them, and re-layouts  48.3 us
    psum x1, waiting for transfers between devices, shards(): lax.psum(as_sent(tuple(shares)), 'replica')  42.7 us
    dot_general x2, matrix products, backward_block(): jnp.einsum('qhd,khd->hqk', grad_block, values, preferred_element_type=jnp...  39.2 us
    unnamed x1, blocking collectives  35.2 us
  transfers between devices with their start and end apart: 12, of which 8 were waited for; matrix products, arithmetic and copies ran while one was open for 21% of the time, Pallas kernels for 0%

commit v1 on v0

--- a/solution.py
+++ b/solution.py
@@ -9,6 +9,19 @@
 HD = 64
 BLK = 64
 norm_eps = 1e-06
+
+
+def ring_gather(value, axis, dim):
+    ways = lax.axis_size(axis)
+    up = [(d, (d + 1) % ways) for d in range(ways)]
+    down = [(d, (d - 1) % ways) for d in range(ways)]
+    earlier, later = ([value], [value])
+    for _ in range(ways // 2):
+        earlier.append(lax.ppermute(earlier[-1], axis, up))
+    for _ in range((ways - 1) // 2):
+        later.append(lax.ppermute(later[-1], axis, down))
+    line = jnp.concatenate([*earlier[::-1], *later[1:]], axis=dim)
+    return jnp.roll(line, (lax.axis_index(axis) - ways // 2) * value.shape[dim], axis=dim)
 
 
 def as_sent(array):
@@ -102,7 +115,7 @@
         lax.all_gather(up_weight, "fsdp", axis=0, tiled=True),
         lax.all_gather(down_weight, "fsdp", axis=0, tiled=True),
         lax.all_gather(proj_bias, "fsdp", axis=1, tiled=True),
-        lax.all_gather(up_bias, "fsdp", axis=0, tiled=True),
+        ring_gather(up_bias, "fsdp", 0),
         lax.all_gather(norm_gain, "fsdp", axis=1, tiled=True),
         lax.all_gather(norm_bias, "fsdp", axis=1, tiled=True),
     )

time: 1210 us -> 1200 us (level)
  blocking collectives: 124 us -> 94.3 us
  starting transfers between devices: 0.48 us -> 16.2 us
    all_gather x1 -> x0, blocking collectives: 25.9 us -> none  [shards(): lax.all_gather(up_bias, 'fsdp', axis=0, tiled=True)]
    ppermute x0 -> x7, starting transfers between devices: none -> 15.7 us  [the longest x3 12.7 us: ring_gather(): later.append(lax.ppermute(later[-1], axis, down))]
    unnamed x126 -> x144, local copies, waits for them, and re-layouts: 48.3 us -> 50.3 us
  transfers between devices with their start and end apart: 12 -> 19, of which waited for: 8 -> 11; matrix products, arithmetic and copies ran while one was open for 21% -> 22% of each run, Pallas kernels for 0% -> 0%
where the time goes in v1:
time: 1200 us
  waiting for transfers between devices  683 us (57%)
  matrix products  233 us (19%)
  other arithmetic  94.5 us (8%)
  blocking collectives  94.3 us (8%)
  local copies, waits for them, and re-layouts  61.2 us (5%)
  between operations  16.4 us (1%)
  starting transfers between devices  16.2 us (1%)
    unnamed x16, waiting for transfers between devices  234 us
    reduce_scatter x1, waiting for transfers between devices, shards(): lax.psum_scatter(down_grad, 'fsdp', scatter_dimension=0, tiled=True)  164 us
    reduce_scatter x1, waiting for transfers between devices, shards(): lax.psum_scatter(up_grad, 'fsdp', scatter_dimension=0, tiled=True)  164 us
    all_gather x1, waiting for transfers between devices, shards(): lax.all_gather(down_weight, 'fsdp', axis=0, tiled=True)  69.1 us
    unnamed x144, local copies, waits for them, and re-layouts  50.3 us
    psum x1, waiting for transfers between devices, shards(): lax.psum(as_sent(tuple(shares)), 'replica')  42.6 us
    dot_general x2, matrix products, backward_block(): jnp.einsum('qhd,khd->hqk', grad_block, values, preferred_element_type=jnp...  39.8 us
    unnamed x1, blocking collectives  35.2 us
  transfers between devices with their start and end apart: 19, of which 11 were waited for; matrix products, arithmetic and copies ran while one was open for 22% of the time, Pallas kernels for 0%

profile of v1, /device:TPU:0, one launch (start us, length us, event | category | flops | bytes accessed | tf_op | source)
XLA Modules:
  0.0 1198.8 jit_solution(7749272504422463578)
XLA Ops:
  9.5 3.0 collective-permute-start
  12.5 3.1 collective-permute-start.4
  17.3 18.3 %all-gather.1 = bf16[8,96,2]{1,2,0:T(2,128)(2,1)S(1)} all-gather(bf16[1,96,2]{1,2,0:T(2,128)(2,1)} %bitcast.134), channel_id=1, replica_groups=mesh['replica'=4,'fsdp'=8] {'fsdp'}, dimensions={0}, use_global_device_ids=true | all-gather | bytes 3456 | tf_op jit(solution)/shard_map/all_gather | solution.py:119
  35.6 16.6 %all-gather.2 = bf16[8,96,2]{1,2,0:T(2,128)(2,1)S(1)} all-gather(bf16[1,96,2]{1,2,0:T(2,128)(2,1)} %bitcast.135), channel_id=1, replica_groups=mesh['replica'=4,'fsdp'=8] {'fsdp'}, dimensions={0}, use_global_device_ids=true | all-gather | bytes 3456 | tf_op jit(solution)/shard_map/all_gather | solution.py:120
  52.3 18.6 %all-gather = bf16[8,96,4]{1,2,0:T(4,128)(2,1)S(1)} all-gather(bf16[1,96,4]{1,2,0:T(4,128)(2,1)} %bitcast.133), channel_id=1, replica_groups=mesh['replica'=4,'fsdp'=8] {'fsdp'}, dimensions={0}, use_global_device_ids=true | all-gather | bytes 6912 | tf_op jit(solution)/shard_map/all_gather | solution.py:117
  74.0 5.7 collective-permute-done.1
  79.7 4.7 collective-permute-start.5
  90.5 2.7 copy.93
  93.2 4.9 collective-permute-start.6
  102.1 5.8 fusion.67
  108.0 3.6 copy-done.17
  112.5 5.1 fusion.21
  120.0 1.7 copy.95
  121.7 12.9 %fusion.20 = (f32[12,512]{1,0:T(8,128)S(1)}, f32[12,512,1024]{2,1,0:T(8,128)}) fusion(pred[512,1024]{1,0:T(8,128)(4,1)} %copy.100, bf16[512,12,64]{0,2,1:T(8,128)(2,1)} %bitcast.107, bf16[1024,12,64]{0,2,1:T(8,128)(2,1)S(1)} %bitcast.99), kind=kOutput, calls=%fused_computation.34 | convolution fusion | flops 824174592 | bytes 28073984 | tf_op jit(solution)/shard_map/qhd,khd->hqk/dot_general | solution.py:58
  134.6 12.7 %fusion.1 = f32[12,512]{1,0:T(8,128)S(1)} fusion(f32[12,512]{1,0:T(8,128)S(1)} %get-tuple-element.103, f32[12,512,1024]{2,1,0:T(8,128)} %get-tuple-element.104, pred[512,1024]{1,0:T(8,128)(4,1)S(1)} %copy-done.13), kind=kLoop, calls=%fused_computation.13 | loop fusion | flops 25159680 | bytes 25739264 | tf_op jit(solution)/shard_map/reduce_sum | solution.py:67
  147.3 2.9 copy-done.1
  150.2 8.4 fusion.32
  158.7 12.0 %fusion.19 = (f32[12,512]{1,0:T(8,128)S(1)}, f32[12,512,1024]{2,1,0:T(8,128)}) fusion(pred[512,1024]{1,0:T(8,128)(4,1)S(1)} %copy-done.10, bf16[512,12,64]{0,2,1:T(8,128)(2,1)} %bitcast.109, bf16[1024,12,64]{0,2,1:T(8,128)(2,1)S(1)} %bitcast.100), kind=kOutput, calls=%fused_computation.33 | convolution fusion | flops 824174592 | bytes 28073984 | tf_op jit(solution)/shard_map/qhd,khd->hqk/dot_general | solution.py:58
  170.7 12.3 %fusion = f32[12,512]{1,0:T(8,128)S(1)} fusion(f32[12,512]{1,0:T(8,128)S(1)} %get-tuple-element.105, f32[12,512,1024]{2,1,0:T(8,128)} %get-tuple-element.106, pred[512,1024]{1,0:T(8,128)(4,1)S(1)} %copy-done.10), kind=kLoop, calls=%fused_computation.12 | loop fusion | flops 25159680 | bytes 25739264 | tf_op jit(solution)/shard_map/reduce_sum | solution.py:67
  183.0 3.1 copy-done
  186.2 7.8 fusion.31
  195.3 3.8 fusion.65
  199.6 1.7 all-gather.12.cloned.1.call-done
  201.3 11.0 fusion.57
  212.3 69.1 %all-gather.14.cloned.1.call-done = bf16[3072,768]{1,0:T(8,128)(2,1)} async-done(((bf16[384,768]{1,0:T(8,128)(2,1)}), bf16[3072,768]{1,0:T(8,128)(2,1)}) %all-gather.14.cloned.1.call-update) | async-done | bytes 4718608 | tf_op jit(solution)/shard_map/all_gather | solution.py:116
  281.4 11.5 fusion.66
  292.9 1.7 multiply_reduce_fusion.5
  294.6 2.1 multiply_reduce_fusion.2
  296.7 3.6 convert_reduce_fusion.1
  300.3 18.2 %convert_reduce_fusion = (f32[3072]{0:T(1024)}, bf16[1024,3072]{1,0:T(8,128)(2,1)}) fusion(f32[1024,3072]{1,0:T(8,128)} %fusion.57, f32[3072]{0:T(1024)S(1)} %copy-done.45, bf16[1024,768]{0,1:T(8,128)(2,1)S(1)} %get-tuple-element.89, bf16[3072,768]{1,0:T(8,128)(2,1)} %all-gather.14.cloned.1.call-done), kind=kOutput, calls=%fused_computation.27 | convolution fusion | flops 4904186880 | bytes 25190400 | tf_op jit(solution)/shard_map/sd,fd->sf/dot_general | solution.py:166
  318.5 9.4 multiply_reduce_fusion.3
  331.3 2.8 fusion.69
  337.3 21.5 %multiply_reduce_fusion.1 = (f32[12,512]{1,0:T(8,128)S(1)}, f32[12,512,1024]{2,1,0:T(8,128)}) fusion(f32[12,512]{1,0:T(8,128)S(1)} %log_add_fusion.1, f32[12,512,1024]{2,1,0:T(8,128)} %get-tuple-element.106, pred[512,1024]{1,0:T(8,128)(4,1)S(1)} %copy-done.11, bf16[512,12,64]{0,2,1:T(8,128)(2,1)S(1)} %bitcast.115, bf16[1024,12,64]{0,2,1:T(8,128)(2,1)S(1)} %bitcast.105), kind=kOutput, calls=%fused_computation.4 | convolution fusion | flops 836757504 | bytes 53264384 | tf_op jit(solution)/shard_map/qhd,khd->hqk/dot_general | solution.py:76
  358.8 17.2 %multiply_convert_fusion.1 = bf16[12,512,1024]{2,1,0:T(8,128)(2,1)S(1)} fusion(f32[12,512,1024]{2,1,0:T(8,128)} %get-tuple-element.113, f32[12,512]{1,0:T(8,128)S(1)} %get-tuple-element.112, f32[12,512]{1,0:T(8,128)S(1)} %log_add_fusion.1, f32[12,512,1024]{2,1,0:T(8,128)} %get-tuple-element.106, pred[512,1024]{1,0:T(8,128)(4,1)} %copy.97), kind=kLoop, calls=%fused_computation.3 | loop fusion | flops 37748736 | bytes 63488000 | tf_op jit(solution)/shard_map/convert_element_type | solution.py:78
  376.0 6.2 multiply_bitcast_fusion.1
  382.3 5.1 fusion.68
  388.7 18.2 %multiply_reduce_fusion = (f32[12,512]{1,0:T(8,128)S(1)}, f32[12,512,1024]{2,1,0:T(8,128)}) fusion(f32[12,512]{1,0:T(8,128)S(1)} %log_add_fusion, f32[12,512,1024]{2,1,0:T(8,128)} %get-tuple-element.104, pred[512,1024]{1,0:T(8,128)(4,1)} %copy.100, bf16[512,12,64]{0,2,1:T(8,128)(2,1)} %bitcast.117, bf16[1024,12,64]{0,2,1:T(8,128)(2,1)S(1)} %bitcast.106), kind=kOutput, calls=%fused_computation.1 | convolution fusion | flops 836757504 | bytes 53264384 | tf_op jit(solution)/shard_map/qhd,khd->hqk/dot_general | solution.py:76
  407.0 17.6 %multiply_convert_fusion = bf16[12,512,1024]{2,1,0:T(8,128)(2,1)S(1)} fusion(f32[12,512,1024]{2,1,0:T(8,128)} %get-tuple-element.115, f32[12,512]{1,0:T(8,128)S(1)} %get-tuple-element.114, f32[12,512]{1,0:T(8,128)S(1)} %log_add_fusion, f32[12,512,1024]{2,1,0:T(8,128)} %get-tuple-element.104, pred[512,1024]{1,0:T(8,128)(4,1)} %copy.100), kind=kLoop, calls=%fused_computation | loop fusion | flops 37748736 | bytes 63488000 | tf_op jit(solution)/shard_map/convert_element_type | solution.py:78
  424.6 6.2 multiply_bitcast_fusion
  430.9 2.9 convert_reduce_fusion.4
  433.8 4.7 multiply_convert_fusion.3
  438.5 11.9 fusion.11
  450.5 12.1 %convert_reduce_fusion.3 = (f32[12,64]{1,0:T(8,128)S(1)}, bf16[12,64,1024]{2,1,0:T(8,128)(2,1)S(1)}) fusion(f32[12,64,1024]{2,1,0:T(8,128)S(1)} %fusion.11, bf16[512,12,64]{0,2,1:T(8,128)(2,1)S(1)} %bitcast.116, f32[12,512]{1,0:T(8,128)S(1)} %log_add_fusion.1, f32[12,512,1024]{2,1,0:T(8,128)} %get-tuple-element.106, pred[512,1024]{1,0:T(8,128)(4,1)S(1)} %copy-done.12), kind=kOutput, calls=%fused_computation.50 | convolution fusion | flops 833617152 | bytes 31222784 | tf_op jit(solution)/shard_map/hqk,qhd->khd/dot_general | solution.py:86
  463.7 9.1 convolution_bitcast_fusion
  472.9 8.0 copy.112
  480.9 1.8 copy-done.4
  482.8 10.5 fusion.55
  494.7 13.9 %fusion.60 = f32[3072,768]{1,0:T(8,128)} fusion(bf16[1024,768]{0,1:T(8,128)(2,1)S(1)} %copy-done.29, f32[1024,3072]{1,0:T(8,128)} %fusion.57, f32[3072]{0:T(1024)S(1)} %copy-done.46), kind=kOutput, calls=%fused_computation.135 | convolution fusion | flops 4863295488 | bytes 23605248 | tf_op jit(solution)/shard_map/sf,sd->fd/dot_general | solution.py:163
  517.1 90.9 %reduce-scatter.22.cloned.1.call-done = f32[96,2304]{1,0:T(8,128)} async-done(((f32[768,2304]{1,0:T(8,128)}), f32[96,2304]{1,0:T(8,128)}) %reduce-scatter.22.cloned.1.call-update) | async-done | bytes 884752
  608.0 2.2 copy.113
  610.2 164.2 %reduce-scatter.18.cloned.1.call-done = f32[96,3072]{1,0:T(8,128)} async-done(((f32[768,3072]{1,0:T(8,128)}), f32[96,3072]{1,0:T(8,128)}) %reduce-scatter.18.cloned.1.call-update) | async-done | bytes 1179664 | tf_op jit(solution)/shard_map/reduce_scatter | solution.py:218
  774.4 2.2 convert_element_type.207
  776.6 164.3 %reduce-scatter.20.cloned.1.call-done = f32[384,768]{1,0:T(8,128)} async-done(((f32[3072,768]{1,0:T(8,128)}), f32[384,768]{1,0:T(8,128)}) %reduce-scatter.20.cloned.1.call-update) | async-done | bytes 1179664 | tf_op jit(solution)/shard_map/reduce_scatter | solution.py:219
  940.9 2.1 convert_element_type.209
  943.1 8.9 add_add_fusion.4
  952.0 3.6 copy.108
  955.5 35.2 %all-reduce = bf16[3072]{0:T(1024)(128)(2,1)S(1)} all-reduce(f32[3072]{0:T(1024)S(1)} %copy-done.44), channel_id=7, replica_groups=mesh['replica'=4,'fsdp'=8] {'fsdp'}, use_global_device_ids=true, to_apply=%region_30.31.clone | all-reduce | flops 3072 | bytes 18432
  990.8 14.3 %reduce-scatter.28.cloned.1.call-done = f32[96,2]{1,0:T(8,128)} async-done(((f32[768,2]{1,0:T(8,128)}), f32[96,2]{1,0:T(8,128)}) %reduce-scatter.28.cloned.1.call-update) | async-done | bytes 784
  1006.0 63.1 %reduce-scatter.26.cloned.1.call-done = f32[96,2]{1,0:T(8,128)} async-done(((f32[768,2]{1,0:T(8,128)}), f32[96,2]{1,0:T(8,128)}) %reduce-scatter.26.cloned.1.call-update) | async-done | bytes 784
  1069.9 63.2 %reduce-scatter.24.cloned.1.call-done = f32[96,4]{1,0:T(8,128)} async-done(((f32[768,4]{1,0:T(8,128)}), f32[96,4]{1,0:T(8,128)}) %reduce-scatter.24.cloned.1.call-update) | async-done | bytes 1552
  1134.0 5.7 all-reduce.1
  1141.9 42.6 %all-reduce.5.cloned.1.call-done = (bf16[96,2304]{0,1:T(8,128)(2,1)}, bf16[96,768]{1,0:T(8,128)(2,1)}, bf16[96,3072]{1,0:T(8,128)(2,1)}, bf16[384,768]{1,0:T(8,128)(2,1)}) async-done(((bf16[96,2304]{0,1:T(8,128)(2,1)}, bf16[96,768]{1,0:T(8,128)(2,1)}, bf16[96,3072]{1,0:T(8,128)(2,1)}, bf16[384,768]{1,0:T(8,128)(2,1)}), (bf16[96,2304]{0,1:T(8,128)(2,1)}, bf16[96,768]{1,0:T(8,128)(2,1)}, ...) | async-done | bytes 1769488 | tf_op jit(solution)/shard_map/psum | solution.py:226
  1184.6 2.3 copy.109
  1188.5 2.2 convert_element_type.208
  (232 shorter events, 47.8 us)
Async XLA Ops:
  7.2 94.9 %all-gather.8.cloned.1.call-start = ((), (), s32[]{:S(2)}) async-start(), calls=%async_computation.7 | async-start | bytes 3981312 | tf_op jit(solution)/shard_map/all_gather | solution.py:113
  7.9 187.4 %all-gather.10.cloned.1.call-start = ((), (), s32[]{:S(2)}) async-start(), calls=%async_computation.8 | async-start | bytes 1327104 | tf_op jit(solution)/shard_map/all_gather | solution.py:114
  8.7 192.6 %all-gather.12.cloned.1.call-start = ((), (), s32[]{:S(2)}) async-start(), calls=%async_computation.9 | async-start | bytes 5308416 | tf_op jit(solution)/shard_map/all_gather | solution.py:115
  9.4 79.5 %copy-start.23 = (bf16[1024,768]{1,0:T(8,128)(2,1)S(1)}, bf16[1024,768]{1,0:T(8,128)(2,1)}, u32[]{:S(2)}) copy-start(bf16[1024,768]{1,0:T(8,128)(2,1)} %param.23) | copy-start | bytes 4718596
  9.4 271.9 %all-gather.14.cloned.1.call-start = ((), (), s32[]{:S(2)}) async-start(), calls=%async_computation.10 | async-start | bytes 5308416 | tf_op jit(solution)/shard_map/all_gather | solution.py:116
  9.5 63.9 %collective-permute-start = (bf16[384]{0:T(512)(128)(2,1)}, bf16[384]{0:T(512)(128)(2,1)S(1)}, u32[]{:S(2)}, u32[]{:S(2)}) collective-permute-start(bf16[384]{0:T(512)(128)(2,1)} %param.20), channel_id=1, source_target_pairs={{0,1},{1,2},{2,3},{3,4},{4,5},{5,6},{6,7},{7,0},{8,9},{9,10},{10,1... | collective-permute-start | bytes 2312 | tf_op jit(solution)/shard_map/ppermute | solution.py:20
  12.5 67.2 %collective-permute-start.4 = (bf16[384]{0:T(512)(128)(2,1)}, bf16[384]{0:T(512)(128)(2,1)S(1)}, u32[]{:S(2)}, u32[]{:S(2)}) collective-permute-start(bf16[384]{0:T(512)(128)(2,1)} %param.20), channel_id=1, source_target_pairs={{0,7},{1,0},{2,1},{3,2},{4,3},{5,4},{6,5},{7,6},{8,15},{9,8},{10,9... | collective-permute-start | bytes 2312 | tf_op jit(solution)/shard_map/ppermute | solution.py:22
  15.6 499.9 %reduce-scatter.16.cloned.1.call-start = ((), (), s32[]{:S(2)}) async-start(), calls=%async_computation.11 | async-start | bytes 2654208 | tf_op jit(solution)/shard_map/reduce_scatter | solution.py:217
  73.4 6.3 collective-permute-start.1
  79.7 6.3 collective-permute-start.2
  79.7 13.6 %collective-permute-start.5 = (bf16[384]{0:T(512)(128)(2,1)S(1)}, bf16[384]{0:T(512)(128)(2,1)S(1)}, u32[]{:S(2)}, u32[]{:S(2)}) collective-permute-start(bf16[384]{0:T(512)(128)(2,1)S(1)} %collective-permute-done.4), channel_id=1, source_target_pairs={{0,7},{1,0},{2,1},{3,2},{4,3},{5,4},{6,5},{7,6},{8,15},{9,8},{10,9... | collective-permute-start | bytes 2312 | tf_op jit(solution)/shard_map/ppermute | solution.py:22
  85.9 12.2 %collective-permute-start.3 = (bf16[384]{0:T(512)(128)(2,1)S(1)}, bf16[384]{0:T(512)(128)(2,1)S(1)}, u32[]{:S(2)}, u32[]{:S(2)}) collective-permute-start(bf16[384]{0:T(512)(128)(2,1)S(1)} %collective-permute-done.2), channel_id=1, source_target_pairs={{0,1},{1,2},{2,3},{3,4},{4,5},{5,6},{6,7},{7,0},{8,9},{9,10},{10,1... | collective-permute-start | bytes 2312 | tf_op jit(solution)/shard_map/ppermute | solution.py:20
  88.9 10.0 copy-start.50
  90.5 11.6 copy-start.24
  93.2 6.3 collective-permute-start.6
  107.9 3.6 copy-start.17
  112.5 46.2 %copy-start.2 = (bf16[1024,768]{0,1:T(8,128)(2,1)}, bf16[1024,768]{0,1:T(8,128)(2,1)S(1)}, u32[]{:S(2)}) copy-start(bf16[1024,768]{0,1:T(8,128)(2,1)S(1)} %copy.99) | copy-start | bytes 4718596
  121.7 61.3 %copy-start.7 = (bf16[1024,768]{0,1:T(8,128)(2,1)}, bf16[1024,768]{0,1:T(8,128)(2,1)S(1)}, u32[]{:S(2)}) copy-start(bf16[1024,768]{0,1:T(8,128)(2,1)S(1)} %copy.95) | copy-start | bytes 4718596
  121.7 12.9 %copy-start.13 = (pred[512,1024]{1,0:T(8,128)(4,1)S(1)}, pred[512,1024]{1,0:T(8,128)(4,1)}, u32[]{:S(2)}) copy-start(pred[512,1024]{1,0:T(8,128)(4,1)} %copy.100) | copy-start | bytes 1572868
  134.6 15.6 %copy-start.1 = (f32[12,512,1024]{2,1,0:T(8,128)S(1)}, f32[12,512,1024]{2,1,0:T(8,128)}, u32[]{:S(2)}) copy-start(f32[12,512,1024]{2,1,0:T(8,128)} %get-tuple-element.104) | copy-start | bytes 75497472
  150.2 8.5 copy-start.10
  170.7 15.5 %copy-start = (f32[12,512,1024]{2,1,0:T(8,128)S(1)}, f32[12,512,1024]{2,1,0:T(8,128)}, u32[]{:S(2)}) copy-start(f32[12,512,1024]{2,1,0:T(8,128)} %get-tuple-element.106) | copy-start | bytes 75497472
  186.2 7.8 copy-start.30
  199.1 128.8 %copy-start.3 = (f32[1024,768]{0,1:T(8,128)}, f32[1024,768]{0,1:T(8,128)S(1)}, u32[]{:S(2)}) copy-start(f32[1024,768]{0,1:T(8,128)S(1)} %get-tuple-element.108) | copy-start | bytes 9437188
  199.1 2.1 copy-start.32
  199.1 2.1 copy-start.33
  201.3 80.1 %copy-start.45 = (f32[3072]{0:T(1024)S(1)}, f32[3072]{0:T(1024)}, u32[]{:S(2)}) copy-start(f32[3072]{0:T(1024)} %dynamic-slice_convert_fusion) | copy-start | bytes 36868
  201.3 80.1 %copy-start.47 = (f32[768]{0:T(1024)S(1)}, f32[768]{0:T(1024)}, u32[]{:S(2)}) copy-start(f32[768]{0:T(1024)} %get-tuple-element.72) | copy-start | bytes 9220
  281.3 11.5 copy-start.6
  281.4 11.6 copy-start.35
  281.4 11.6 copy-start.36
  294.6 2.1 copy-start.37
  296.7 21.8 %slice-start = ((s8[4718592]{0:T(1024)(128)(4,1)}), s8[4194304]{0:T(1024)(128)(4,1)S(1)}, s32[]{:S(2)}) async-start(s8[4718592]{0:T(1024)(128)(4,1)} %bitcast.111), calls=%async_computation.19 | async-start | bytes 8388608
  300.3 18.2 %copy-start.28 = (bf16[1024,768]{0,1:T(8,128)(2,1)}, bf16[1024,768]{0,1:T(8,128)(2,1)S(1)}, u32[]{:S(2)}) copy-start(bf16[1024,768]{0,1:T(8,128)(2,1)S(1)} %get-tuple-element.89) | copy-start | bytes 4718596
  300.3 18.2 %slice-start.1 = ((s8[4718592]{0:T(1024)(128)(4,1)}), s8[524288]{0:T(1024)(128)(4,1)S(1)}, s32[]{:S(2)}) async-start(s8[4718592]{0:T(1024)(128)(4,1)} %bitcast.111), calls=%async_computation.20 | async-start | bytes 1048576
  328.7 2.6 copy-start.27
  328.8 5.4 copy-start.41
  331.3 2.8 copy-start.51
  335.5 1.8 copy-start.11
  336.5 22.3 %copy-start.20 = (bf16[512,768]{0,1:T(8,128)(2,1)}, bf16[512,768]{0,1:T(8,128)(2,1)S(1)}, u32[]{:S(2)}) copy-start(bf16[512,768]{0,1:T(8,128)(2,1)S(1)} %get-tuple-element.95) | copy-start | bytes 2359300
  387.4 220.7 %reduce-scatter.22.cloned.1.call-start = ((), (), s32[]{:S(2)}) async-start(), calls=%async_computation.14 | async-start | bytes 7962624
  430.9 2.9 copy-start.5
  433.8 4.8 copy-start.14
  433.8 4.8 copy-start.22
  438.5 11.9 copy-start.12
  438.5 11.9 copy-start.21
  450.5 13.3 %copy-start.19 = (bf16[12,64,1024]{2,1,0:T(8,128)(2,1)S(1)}, bf16[12,64,1024]{2,1,0:T(8,128)(2,1)}, u32[]{:S(2)}) copy-start(bf16[12,64,1024]{2,1,0:T(8,128)(2,1)} %multiply_convert_fusion.3) | copy-start | bytes 4718596
  450.5 13.2 %copy-start.25 = (bf16[1024,768]{1,0:T(8,128)(2,1)S(1)}, bf16[1024,768]{1,0:T(8,128)(2,1)}, u32[]{:S(2)}) copy-start(bf16[1024,768]{1,0:T(8,128)(2,1)} %param.12) | copy-start | bytes 4718596
  450.5 13.2 %copy-start.26 = (bf16[1024,12,64]{0,2,1:T(8,128)(2,1)S(1)}, bf16[1024,12,64]{0,2,1:T(8,128)(2,1)}, u32[]{:S(2)}) copy-start(bf16[1024,12,64]{0,2,1:T(8,128)(2,1)} %get-tuple-element.85) | copy-start | bytes 4718596
  480.9 1.9 copy-start.4
  480.9 1.9 copy-start.34
  480.9 293.5 %reduce-scatter.18.cloned.1.call-start = ((), (), s32[]{:S(2)}) async-start(), calls=%async_computation.12 | async-start | bytes 10616832 | tf_op jit(solution)/shard_map/reduce_scatter | solution.py:218
  493.3 447.6 %reduce-scatter.20.cloned.1.call-start = ((), (), s32[]{:S(2)}) async-start(), calls=%async_computation.13 | async-start | bytes 10616832 | tf_op jit(solution)/shard_map/reduce_scatter | solution.py:219
  508.6 2.8 copy-start.40
  508.6 4.0 copy-start.53
  508.7 5.3 copy-start.18
  508.7 496.4 %reduce-scatter.28.cloned.1.call-start = ((), (), s32[]{:S(2)}) async-start(), calls=%async_computation.17 | async-start | bytes 442368
  510.3 558.7 %reduce-scatter.26.cloned.1.call-start = ((), (), s32[]{:S(2)}) async-start(), calls=%async_computation.16 | async-start | bytes 442368
  511.5 621.6 %reduce-scatter.24.cloned.1.call-start = ((), (), s32[]{:S(2)}) async-start(), calls=%async_computation.15 | async-start | bytes 442368
  512.6 672.0 %all-reduce.5.cloned.1.call-start = ((), (), s32[]{:S(2)}) async-start(), calls=%async_computation.18 | async-start | bytes 3833856 | tf_op jit(solution)/shard_map/psum | solution.py:226
  517.1 425.9 %copy-start.16 = (f32[1024,768]{0,1:T(8,128)S(1)}, f32[1024,768]{0,1:T(8,128)}, u32[]{:S(2)}) copy-start(f32[1024,768]{0,1:T(8,128)} %copy-done.15) | copy-start | bytes 9437188
  517.1 426.0 %copy-start.42 = (f32[1024]{0:T(1024)S(1)}, f32[1024]{0:T(1024)}, u32[]{:S(2)}) copy-start(f32[1024]{0:T(1024)} %copy-done.41) | copy-start | bytes 12292
  952.0 3.6 copy-start.44
  1184.6 6.1 copy-start.31
  (11 other events, 13.3 us)
Sparse Core Ops, SparseCore 0:
  10.2 68.0 all-gather.7
  80.4 39.7 all-gather.9
  122.4 78.7 all-gather.11
  203.3 78.0 all-gather.13
  387.5 67.2 reduce-scatter.15
  481.0 126.9 reduce-scatter.21
  612.0 162.3 reduce-scatter.17
  778.4 162.4 reduce-scatter.19
  944.5 60.5 reduce-scatter.27
  1008.6 60.4 reduce-scatter.25
  1072.6 60.4 reduce-scatter.23
  1136.4 48.1 all-reduce.4
